TPU v7x, 32 devices: a whole 2x2x4 slice. The times are simulated.
32 devices in a mesh: batch: 8 (over y, x, core), tile: 4 (over z).
Axes of the slice: x: 2, y: 2, z: 4, core: 2. Of those that a mesh axis runs over, the one named last changes fastest.
Arguments:
- object_field: float32 [2, 2, 3072, 1536], P(None, None, 'batch', 'tile'), may hold values from -6 to 6
- probe_wave: bfloat16 [2, 256, 256], replicated, may hold values from -4.1875 to 4.1875
- intensities: float32 [512, 256, 256], P(('batch', 'tile')), may hold values from 0 to 4
- owner_rows: int32 [512, 1], P(('batch', 'tile')), may hold values from 0 to 7; in each aligned block of 16 rows (0 to 15, 16 to 31, ...) at most 4 rows name the same one
- offsets: int32 [512, 2], P(('batch', 'tile')), may hold values from 0 to 128
Outputs:
- new_object: float32 [2, 2, 3072, 1536], P(None, None, 'batch', 'tile')
- new_probe: float32 [2, 256, 256], replicated
Inputs may be any that keep to these rules, and one draw needn't show every extreme that they name: `owner_rows`: within the 16 positions of one device, each tile row is named at most 4 times.
All inputs are finite; a program needn't handle non-finite values.
Results may differ from a plain program's by a relative error of at most 0.008.
The roundings to bfloat16 on the way count: a program that leaves them out, or rounds other values in their place, can miss the bound.
Values may be sent and summed in bfloat16 or wider, within the bound.
A program may use at most 192 MiB of HBM per device.

v0:
```python
import math

import jax
import jax.numpy as jnp
from jax import lax
from jax.sharding import PartitionSpec as P

update_rate = 0.1
tv_weight = 12.0
tv_smooth = 1.0
probe_rate = 0.04


def extended(x, sides, width):
    for axis, dim in sides:
        size, length = (lax.axis_size(axis), x.shape[dim])
        up = [(i, (i + 1) % size) for i in range(size)]
        down = [(j, i) for i, j in up]
        last = lax.slice_in_dim(x, length - width, length, axis=dim)
        first = lax.slice_in_dim(x, 0, width, axis=dim)
        before = lax.ppermute(last, axis, up)
        after = lax.ppermute(first, axis, down)
        x = jnp.concatenate([before, x, after], axis=dim)
    return x


def tables(extent):
    counter = jnp.arange(extent, dtype=jnp.int32)
    product = counter[:, None] * counter[None, :] % extent
    angles = product.astype(jnp.float32) * (2.0 * math.pi / extent)
    scaling = 1.0 / math.sqrt(extent)
    cos_table = (jnp.cos(angles) * scaling).astype(jnp.bfloat16)
    sin_table = (-jnp.sin(angles) * scaling).astype(jnp.bfloat16)
    frequency = (counter + extent // 2) % extent - extent // 2
    squared = (frequency * frequency).astype(jnp.float32)
    phases = -(0.5 / extent) * (squared[:, None] + squared[None, :])
    return (cos_table, sin_table, jnp.cos(phases), jnp.sin(phases))


def transform(real_part, imag_part, cos_table, sin_table):
    extent = real_part.shape[0]
    left_stack = jnp.concatenate([cos_table, sin_table], 0)
    right_stack = jnp.concatenate([real_part, imag_part], 1)
    blocks = jnp.dot(left_stack, right_stack, preferred_element_type=jnp.float32)
    mid_real = (blocks[:extent, :extent] - blocks[extent:, extent:]).astype(jnp.bfloat16)
    mid_imag = (blocks[:extent, extent:] + blocks[extent:, :extent]).astype(jnp.bfloat16)
    left_two = jnp.concatenate([mid_real, mid_imag], 0)
    right_two = jnp.concatenate([cos_table, sin_table], 1)
    second = jnp.dot(left_two, right_two, preferred_element_type=jnp.float32)
    out_real = second[:extent, :extent] - second[extent:, extent:]
    out_imag = second[:extent, extent:] + second[extent:, :extent]
    return (out_real, out_imag)


def multislice(object_patch, probe_wave, measured, cos_table, sin_table, prop_real, prop_imag):
    slices = object_patch.shape[0]
    back_sin = -sin_table
    psi_real = probe_wave[0]
    psi_imag = probe_wave[1]
    entering = []
    for slab_index in range(slices):
        trans_real = object_patch[slab_index, 0].astype(jnp.float32)
        trans_imag = object_patch[slab_index, 1].astype(jnp.float32)
        entering.append((psi_real, psi_imag))
        wave_real = psi_real.astype(jnp.float32)
        wave_imag = psi_imag.astype(jnp.float32)
        prod_real = (wave_real * trans_real - wave_imag * trans_imag).astype(jnp.bfloat16)
        prod_imag = (wave_real * trans_imag + wave_imag * trans_real).astype(jnp.bfloat16)
        if slab_index + 1 < slices:
            far_real, far_imag = transform(prod_real, prod_imag, cos_table, sin_table)
            kick_real = (prop_real * far_real - prop_imag * far_imag).astype(jnp.bfloat16)
            kick_imag = (prop_real * far_imag + prop_imag * far_real).astype(jnp.bfloat16)
            near_real, near_imag = transform(kick_real, kick_imag, cos_table, back_sin)
            psi_real = near_real.astype(jnp.bfloat16)
            psi_imag = near_imag.astype(jnp.bfloat16)
    exit_real, exit_imag = transform(prod_real, prod_imag, cos_table, sin_table)
    misfit = 0.5 * (exit_real * exit_real + exit_imag * exit_imag - measured)
    chi_real = (misfit * exit_real).astype(jnp.bfloat16)
    chi_imag = (misfit * exit_imag).astype(jnp.bfloat16)
    grad_real, grad_imag = transform(chi_real, chi_imag, cos_table, back_sin)
    object_grads = [None] * slices
    for slab_index in reversed(range(slices)):
        trans_real = object_patch[slab_index, 0].astype(jnp.float32)
        trans_imag = object_patch[slab_index, 1].astype(jnp.float32)
        wave_real = entering[slab_index][0].astype(jnp.float32)
        wave_imag = entering[slab_index][1].astype(jnp.float32)
        object_grads[slab_index] = jnp.stack(
            [
                grad_real * wave_real + grad_imag * wave_imag,
                grad_imag * wave_real - grad_real * wave_imag,
            ]
        )
        dpsi_real = grad_real * trans_real + grad_imag * trans_imag
        dpsi_imag = grad_imag * trans_real - grad_real * trans_imag
        if slab_index > 0:
            back_real, back_imag = transform(
                dpsi_real.astype(jnp.bfloat16), dpsi_imag.astype(jnp.bfloat16), cos_table, back_sin
            )
            turn_real = (prop_real * back_real + prop_imag * back_imag).astype(jnp.bfloat16)
            turn_imag = (prop_real * back_imag - prop_imag * back_real).astype(jnp.bfloat16)
            grad_real, grad_imag = transform(turn_real, turn_imag, cos_table, sin_table)
    patch_grad = jnp.stack(object_grads).astype(jnp.bfloat16)
    probe_grad = jnp.stack([dpsi_real, dpsi_imag])
    return (patch_grad, probe_grad)


def tv_local(padded):
    corner_cells = padded[:, :, :-1, :-1]
    down_diff = padded[:, :, 1:, :-1] - corner_cells
    right_diff = padded[:, :, :-1, 1:] - corner_cells
    weight = 1.0 / jnp.sqrt(
        jnp.sum(down_diff * down_diff + right_diff * right_diff, axis=1, keepdims=True) + tv_smooth
    )
    flow_down = weight * down_diff
    flow_right = weight * right_diff
    return (
        flow_down[:, :, :-1, 1:]
        + flow_right[:, :, 1:, :-1]
        - flow_down[:, :, 1:, 1:]
        - flow_right[:, :, 1:, 1:]
    )


def on_device(object_field, probe_wave, intensities, owner_rows, offsets):
    slices = object_field.shape[0]
    tile_rows = object_field.shape[2]
    extent = probe_wave.shape[-1]
    local_rows = intensities.shape[0]
    nbatch = lax.axis_size("batch")
    capacity = max(2, 2 * local_rows // nbatch)
    slots_all = nbatch * capacity
    patch_shape = (slices, 2, extent, extent)
    targets = owner_rows[:, 0]
    serial = jnp.arange(local_rows, dtype=jnp.int32)
    earlier = (targets[:, None] == targets[None, :]) & (serial[None, :] < serial[:, None])
    ranks = jnp.sum(earlier.astype(jnp.int32), axis=1)
    slot_of = targets * capacity + ranks
    request = (
        jnp.zeros((slots_all, 2), jnp.int32).at[slot_of].set(offsets).reshape(nbatch, capacity, 2)
    )
    wanted = lax.all_to_all(request, "batch", split_axis=0, concat_axis=0, tiled=True).reshape(
        slots_all, 2
    )
    anchor = jnp.zeros((), jnp.int32)
    column = lax.all_gather(object_field.astype(jnp.bfloat16), "batch", axis=2, tiled=True)

    def cut_column(target, corner):
        return lax.dynamic_slice(
            column, (anchor, anchor, target * tile_rows + corner[0], corner[1]), patch_shape
        )

    patches_here = jax.vmap(cut_column)(targets, offsets)
    cos_table, sin_table, prop_real, prop_imag = tables(extent)

    def visit_one(probe_local, inputs):
        object_patch, measured = inputs
        patch_grad, probe_grad = multislice(
            object_patch, probe_wave, measured, cos_table, sin_table, prop_real, prop_imag
        )
        return (probe_local + probe_grad, patch_grad)

    probe_local, patch_grads = lax.scan(
        visit_one, jnp.zeros((2, extent, extent), jnp.float32), (patches_here, intensities)
    )
    outgoing = jnp.zeros((slots_all,) + patch_shape, jnp.bfloat16).at[slot_of].set(patch_grads)
    outgoing = outgoing.reshape((nbatch, capacity) + patch_shape)
    returned = lax.all_to_all(outgoing, "batch", split_axis=0, concat_axis=0, tiled=True).reshape(
        (slots_all,) + patch_shape
    )

    def add_slot(slot_idx, field_grad):
        corner = wanted[slot_idx]
        start = (anchor, anchor, corner[0], corner[1])
        current = lax.dynamic_slice(field_grad, start, patch_shape)
        return lax.dynamic_update_slice(
            field_grad, current + returned[slot_idx].astype(jnp.float32), start
        )

    field_grad = lax.fori_loop(0, slots_all, add_slot, jnp.zeros(object_field.shape, jnp.float32))
    probe_total = lax.psum(probe_local, ("batch", "tile"))
    padded = extended(object_field, (("batch", 2), ("tile", 3)), 1)
    new_object = object_field - update_rate * (field_grad + tv_weight * tv_local(padded))
    new_probe = probe_wave.astype(jnp.float32) - probe_rate * probe_total
    return (new_object, new_probe)


def solution(mesh):
    return jax.shard_map(
        on_device,
        mesh=mesh,
        in_specs=(
            P(None, None, "batch", "tile"),
            P(),
            P(("batch", "tile"), None, None),
            P(("batch", "tile"), None),
            P(("batch", "tile"), None),
        ),
        out_specs=(P(None, None, "batch", "tile"), P()),
        check_vma=False,
    )
```

profile of v0, /device:TPU:12, one launch (start us, length us, event | category | flops | bytes accessed | tf_op | source)
XLA Modules:
  0.0 1375.7 jit_solution(8575923773611135377)
XLA Ops:
  18.4 51.6 %all-gather.2.cloned.1.call-done = bf16[2,2,3072,384]{3,2,1,0:T(8,128)(2,1)} async-done(((bf16[2,2,384,384]{3,2,1,0:T(8,128)(2,1)}), bf16[2,2,3072,384]{3,2,1,0:T(8,128)(2,1)}) %all-gather.2.cloned.1.call-update) | async-done | bytes 9437200 | tf_op jit(solution)/shard_map/all_gather | solution.py:145
  74.3 67.6 %while.33 = (s32[]{:T(128)}, bf16[2,2,3072,384]{3,2,1,0:T(8,128)(2,1)}, s32[16,4]{0,1:T(4,128)S(1)}, bf16[16,2,2,256,256]{4,3,2,1,0:T(8,128)(2,1)}, s32[]{:T(128)}) while((s32[]{:T(128)}, bf16[2,2,3072,384]{3,2,1,0:T(8,128)(2,1)}, s32[16,4]{0,1:T(4,128)S(1)}, bf16[16,2,2,256,256]{4,3,2,1,0:T(8,128)(2,1)}, s32[]{:T(128)}) %tuple.156), condition=%wide.while_cond, body=%wide.while_body.sunk | while | flops 2 | bytes 1050225 | solution.py:148
  146.2 224.0 %while.34 = (s32[]{:T(128)}, f32[2,256,256]{1,2,0:T(8,128)}, bf16[16,2,2,256,256]{4,3,2,1,0:T(8,128)(2,1)}, bf16[2,256,256]{1,2,0:T(8,128)(2,1)S(1)}, bf16[16,2,...) while((s32[]{:T(128)}, f32[2,256,256]{1,2,0:T(8,128)}, ...), condition=%wide.region_3.4_spmd.clone.clone.clone.clone, body=%wide.region_2.3_spmd.clone.clone.clone.clone.sunk | while | flops 1626800128 | bytes 54268612 | solution.py:162
  376.1 21.4 %scatter_fusion = bf16[32,2,2,256,256]{4,3,2,1,0:T(8,128)(2,1)} fusion(bf16[32,2,2,256,256]{4,3,2,1,0:T(8,128)(2,1)} %broadcast_in_dim.13, s32[16]{0:T(128)S(1)} %get-tuple-element.547, bf16[16,2,2,256,256]{4,3,2,1,0:T(8,128)(2,1)} %get-tuple-element.229), kind=kCustom, calls=%fused_computation.1 | custom fusion | bytes 25165888 | tf_op jit(solution)/shard_map/scatter | solution.py:165
  410.0 176.2 %collective-permute-done = f32[2,2,1,384]{3,1,2,0:T(2,128)S(1)} collective-permute-done((f32[2,2,1,384]{3,1,2,0:T(2,128)S(1)}, f32[2,2,1,384]{3,1,2,0:T(2,128)S(1)}, u32[]{:S(2)}, u32[]{:S(2)}) %collective-permute-start) | collective-permute-done | bytes 6176 | tf_op jit(solution)/shard_map/ppermute | solution.py:21
  612.5 124.7 %all-reduce.2.cloned.1.call-done = f32[2,256,256]{2,1,0:T(8,128)} async-done(((f32[2,256,256]{2,1,0:T(8,128)}), f32[2,256,256]{2,1,0:T(8,128)}) %all-reduce.2.cloned.1.call-update) | async-done | bytes 524304 | tf_op jit(solution)/shard_map/psum | solution.py:180
  740.6 618.5 %while.32 = (s32[]{:T(128)}, f32[2,2,384,384]{2,3,1,0:T(8,128)}, s32[32,2]{0,1:T(2,128)S(1)}, bf16[32,2,2,256,256]{4,3,2,1,0:T(8,128)(2,1)}, s32[]{:T(128)}, /*index=5*/s32[]{:T(128)}, s32[]{:T(128)}) while((s32[]{:T(128)}, f32[2,2,384,384]{2,3,1,0:T(8,128)}, s32[32,2]{0,1:T(2,128)S(1)}, bf16[32,2,2,256,256]{4,3,2,1,0:T(8,128)(2,1)}, ...), condition=%wide.region_6.7_spmd, body=%wide.region_5.6_spmd.sunk | while | flops 524296 | bytes 11010245 | solution.py:179
  748.5 11.4 dynamic_update_slice.20
  767.8 11.5 dynamic_update_slice.20
  787.2 11.4 dynamic_update_slice.20
  806.5 11.6 dynamic_update_slice.20
  826.0 11.6 dynamic_update_slice.20
  845.5 11.6 dynamic_update_slice.20
  865.1 11.2 dynamic_update_slice.20
  921.5 11.2 dynamic_update_slice.20
  940.7 11.7 dynamic_update_slice.20
  960.3 11.7 dynamic_update_slice.20
  1018.0 11.6 dynamic_update_slice.20
  1037.5 11.5 dynamic_update_slice.20
  1075.9 11.6 dynamic_update_slice.20
  1095.5 11.6 dynamic_update_slice.20
  1114.9 11.6 dynamic_update_slice.20
  1134.5 11.6 dynamic_update_slice.20
  1153.9 11.6 dynamic_update_slice.20
  1173.4 11.6 dynamic_update_slice.20
  1192.9 11.6 dynamic_update_slice.20
  1231.5 11.7 dynamic_update_slice.20
  1251.1 11.2 dynamic_update_slice.20
  1270.2 11.7 dynamic_update_slice.20
  1289.8 11.5 dynamic_update_slice.20
  1328.3 11.7 dynamic_update_slice.20
  1347.9 11.2 dynamic_update_slice.20
  (971 shorter events, 578.4 us)
Async XLA Ops:
  7.2 2.9 copy-start.6
  7.2 3.0 copy-start.7
  7.2 8.8 copy-start.4
  7.2 62.8 %all-gather.2.cloned.1.call-start = ((), (), s32[]{:S(2)}) async-start(), calls=%async_computation.2 | async-start | bytes 10616832 | tf_op jit(solution)/shard_map/all_gather | solution.py:145
  11.8 385.7 %all-to-all-start = ((s32[8,4,2]{1,2,0:T(2,128)}), s32[8,4,2]{1,2,0:T(2,128)S(1)}, u32[]{:S(2)}, u32[]{:S(2)}) async-start(s32[8,4,2]{1,2,0:T(2,128)} %copy.81), calls=%async_computation | async-start | bytes 16384 | tf_op jit(solution)/shard_map/all_to_all | solution.py:141
  157.9 1.3 copy-start.1
  159.4 0.8 copy-start.2
  171.9 1.3 copy-start.1
  173.4 0.8 copy-start.2
  185.9 1.3 copy-start.1
  199.9 1.3 copy-start.1
  213.9 1.3 copy-start.1
  227.9 1.3 copy-start.1
  241.9 1.3 copy-start.1
  255.9 1.3 copy-start.1
  269.9 1.3 copy-start.1
  283.9 1.3 copy-start.1
  297.9 1.3 copy-start.1
  311.8 1.3 copy-start.1
  325.9 1.3 copy-start.1
  339.9 1.3 copy-start.1
  353.8 1.4 copy-start.1
  367.9 1.3 copy-start.1
  397.5 6.7 copy-start
  397.5 341.6 %all-to-all-start.1 = ((bf16[8,4,2,2,256,256]{5,4,3,2,1,0:T(8,128)(2,1)}), bf16[8,4,2,2,256,256]{5,4,3,2,1,0:T(8,128)(2,1)}, u32[]{:S(2)}, u32[]{:S(2)}) async-start(bf16[8,4,2,2,256,256]{5,4,3,2,1,0:T(8,128)(2,1)} %bitcast.219), calls=%async_computation.1 | async-start | bytes 33554432 | tf_op jit(solution)/shard_map/all_to_all | solution.py:167
  404.2 333.0 %all-reduce.2.cloned.1.call-start = ((), (), s32[]{:S(2)}) async-start(), calls=%async_computation.3 | async-start | bytes 1048576 | tf_op jit(solution)/shard_map/psum | solution.py:180
  404.2 182.0 %collective-permute-start = (f32[2,2,1,384]{3,1,2,0:T(2,128)S(1)}, f32[2,2,1,384]{3,1,2,0:T(2,128)S(1)}, u32[]{:S(2)}, u32[]{:S(2)}) collective-permute-start(f32[2,2,1,384]{3,1,2,0:T(2,128)S(1)} %copy.111), channel_id=1, source_target_pairs={{0,4},{4,8},{8,12},{12,16},{16,20},{20,24},{24,28},{28,0},{1,5},{5... | collective-permute-start | bytes 18440 | tf_op jit(solution)/shard_map/ppermute | solution.py:21
  404.4 182.3 %collective-permute-start.1 = (f32[2,2,1,384]{3,1,2,0:T(2,128)S(1)}, f32[2,2,1,384]{3,1,2,0:T(2,128)S(1)}, u32[]{:S(2)}, u32[]{:S(2)}) collective-permute-start(f32[2,2,1,384]{3,1,2,0:T(2,128)S(1)} %copy.112), channel_id=1, source_target_pairs={{4,0},{8,4},{12,8},{16,12},{20,16},{24,20},{28,24},{0,28},{5,1},{9... | collective-permute-start | bytes 18440 | tf_op jit(solution)/shard_map/ppermute | solution.py:22
  594.6 1.7 copy-start.3
  596.2 6.6 collective-permute-start.2
  597.7 5.1 collective-permute-start.3
  607.9 129.2 %copy-start.5 = (bf16[2,256,256]{2,1,0:T(8,128)(2,1)S(1)}, bf16[2,256,256]{2,1,0:T(8,128)(2,1)}, u32[]{:S(2)}) copy-start(bf16[2,256,256]{2,1,0:T(8,128)(2,1)} %param.10) | copy-start | bytes 786436
  (14 other events, 11.1 us)
Sparse Core Ops, SparseCore 0:
  10.5 59.4 all-gather.1
  608.1 129.0 all-reduce.1
where the time goes:
time: 1390 us; the launch traced here: 1380 us
  local copies, waits for them, and re-layouts  664 us (48%)
  waiting for transfers between devices  352 us (25%)
  other arithmetic  143 us (10%)
  loops' own time  121 us (9%)
  matrix products  64.9 us (5%)
  starting transfers between devices  15.7 us (1%)
  between operations  14.2 us (1%)
    dynamic_update_slice x64, local copies, waits for them, and re-layouts, add_slot(): lax.dynamic_update_slice(field_grad, current + returned[slot_idx].astype(...  375 us
    ppermute x2, waiting for transfers between devices, extended(): before = lax.ppermute(last, axis, up)  176 us
    psum x1, waiting for transfers between devices, on_device(): probe_total = lax.psum(probe_local, ('batch', 'tile'))  125 us
    another operation x1, loops' own time, on_device(): lax.fori_loop(0, slots_all, add_slot, jnp.zeros(object_field.shape, jnp.f...  118 us
    gather x48, local copies, waits for them, and re-layouts  67.5 us
    dynamic_slice x64, local copies, waits for them, and re-layouts, add_slot(): current = lax.dynamic_slice(field_grad, start, patch_shape)  67.5 us
    all_gather x1, waiting for transfers between devices, on_device(): lax.all_gather(object_field.astype(jnp.bfloat16), 'batch', axis=2, tiled=...  51.6 us
    dynamic_slice x64, local copies, waits for them, and re-layouts, on_device(): lax.scan(visit_one, jnp.zeros((2, extent, extent), jnp.float32), (patches...  49.4 us
  transfers between devices with their start and end apart: 8, of which 3 were waited for; matrix products, arithmetic and copies ran while one was open for 25% of the time, Pallas kernels for 0%

commit v1 on v0

v1 whole, which is shorter than its diff:
```python
import math

import jax
import jax.numpy as jnp
from jax import lax
from jax.experimental import pallas as pl
from jax.experimental.pallas import tpu as pltpu
from jax.sharding import PartitionSpec as P

update_rate = 0.1
tv_weight = 12.0
tv_smooth = 1.0
probe_rate = 0.04
sublanes = 8


def extended(x, sides, width):
    for axis, dim in sides:
        size, length = (lax.axis_size(axis), x.shape[dim])
        up = [(i, (i + 1) % size) for i in range(size)]
        down = [(j, i) for i, j in up]
        last = lax.slice_in_dim(x, length - width, length, axis=dim)
        first = lax.slice_in_dim(x, 0, width, axis=dim)
        before = lax.ppermute(last, axis, up)
        after = lax.ppermute(first, axis, down)
        x = jnp.concatenate([before, x, after], axis=dim)
    return x


def tables(extent):
    counter = jnp.arange(extent, dtype=jnp.int32)
    product = counter[:, None] * counter[None, :] % extent
    angles = product.astype(jnp.float32) * (2.0 * math.pi / extent)
    scaling = 1.0 / math.sqrt(extent)
    cos_table = (jnp.cos(angles) * scaling).astype(jnp.bfloat16)
    sin_table = (-jnp.sin(angles) * scaling).astype(jnp.bfloat16)
    frequency = (counter + extent // 2) % extent - extent // 2
    squared = (frequency * frequency).astype(jnp.float32)
    phases = -(0.5 / extent) * (squared[:, None] + squared[None, :])
    return (cos_table, sin_table, jnp.cos(phases), jnp.sin(phases))


def transform(real_part, imag_part, left_table, right_table):
    extent = real_part.shape[0]
    stacked = jnp.concatenate([real_part, imag_part], 0)
    mid = jnp.dot(left_table, stacked, preferred_element_type=jnp.float32).astype(jnp.bfloat16)
    second = jnp.dot(
        jnp.concatenate([mid[:extent], mid[extent:]], 1),
        right_table,
        preferred_element_type=jnp.float32,
    )
    return (second[:, :extent], second[:, extent:])


def visit_kernel(
    plan_ref,
    tile_ref,
    measured_ref,
    probe_ref,
    fore_ref,
    back_ref,
    prop_ref,
    sums_ref,
    total_ref,
    wide,
    summed,
    trans,
    psi,
    total,
):
    step = pl.program_id(0)
    slices = tile_ref.shape[1]
    tile_cols = tile_ref.shape[-1]
    extent = probe_ref.shape[-1]
    last_step = pl.num_programs(0) - 1
    opens = plan_ref[1, step] == 0

    @pl.when(step == 0)
    def _():
        total[...] = jnp.zeros_like(total)

    @pl.when(opens)
    def _():
        wide[:, :, : tile_ref.shape[3], :] = tile_ref[0].astype(jnp.float32)
        summed[...] = jnp.zeros_like(summed)

    @pl.when(jnp.logical_not(opens))
    def _():
        row_at = plan_ref[3, step]
        col_at = plan_ref[4, step]
        back_shift = lax.rem(tile_cols - col_at, tile_cols)
        span = extent + sublanes
        row_rest = lax.rem(row_at, sublanes)
        rows = pl.ds(pl.multiple_of(row_at - row_rest, sublanes), span)
        row_shift = lax.rem(span - row_rest, span)
        fore = fore_ref[...]
        back = back_ref[...]

        def add_grad(slab, part, value):
            value = value.astype(jnp.bfloat16).astype(jnp.float32)
            below = jnp.zeros((sublanes, extent), jnp.float32)
            beside = jnp.zeros((span, tile_cols - extent), jnp.float32)
            value = pltpu.roll(jnp.concatenate([value, below], 0), row_rest, 0)
            placed = pltpu.roll(jnp.concatenate([value, beside], 1), col_at, 1)
            summed[slab, part, rows, :] = summed[slab, part, rows, :] + placed

        for slab in range(slices):
            for part in range(2):
                cut = pltpu.roll(wide[slab, part, rows, :], back_shift, 1)[:, :extent]
                trans[slab, part] = pltpu.roll(cut, row_shift, 0)[:extent]
        psi[0] = probe_ref[...]
        for slab in range(slices):
            wave_real = psi[slab, 0].astype(jnp.float32)
            wave_imag = psi[slab, 1].astype(jnp.float32)
            trans_real = trans[slab, 0]
            trans_imag = trans[slab, 1]
            prod_real = (wave_real * trans_real - wave_imag * trans_imag).astype(jnp.bfloat16)
            prod_imag = (wave_real * trans_imag + wave_imag * trans_real).astype(jnp.bfloat16)
            far_real, far_imag = transform(prod_real, prod_imag, fore, back)
            if slab + 1 < slices:
                prop_real = prop_ref[0]
                prop_imag = prop_ref[1]
                kick_real = (prop_real * far_real - prop_imag * far_imag).astype(jnp.bfloat16)
                kick_imag = (prop_real * far_imag + prop_imag * far_real).astype(jnp.bfloat16)
                near_real, near_imag = transform(kick_real, kick_imag, back, fore)
                psi[slab + 1, 0] = near_real.astype(jnp.bfloat16)
                psi[slab + 1, 1] = near_imag.astype(jnp.bfloat16)
        misfit = 0.5 * (far_real * far_real + far_imag * far_imag - measured_ref[0])
        chi_real = (misfit * far_real).astype(jnp.bfloat16)
        chi_imag = (misfit * far_imag).astype(jnp.bfloat16)
        grad_real, grad_imag = transform(chi_real, chi_imag, back, fore)
        for slab in reversed(range(slices)):
            wave_real = psi[slab, 0].astype(jnp.float32)
            wave_imag = psi[slab, 1].astype(jnp.float32)
            trans_real = trans[slab, 0]
            trans_imag = trans[slab, 1]
            add_grad(slab, 0, grad_real * wave_real + grad_imag * wave_imag)
            add_grad(slab, 1, grad_imag * wave_real - grad_real * wave_imag)
            dpsi_real = grad_real * trans_real + grad_imag * trans_imag
            dpsi_imag = grad_imag * trans_real - grad_real * trans_imag
            if slab > 0:
                back_real, back_imag = transform(
                    dpsi_real.astype(jnp.bfloat16), dpsi_imag.astype(jnp.bfloat16), back, fore
                )
                prop_real = prop_ref[0]
                prop_imag = prop_ref[1]
                turn_real = (prop_real * back_real + prop_imag * back_imag).astype(jnp.bfloat16)
                turn_imag = (prop_real * back_imag - prop_imag * back_real).astype(jnp.bfloat16)
                grad_real, grad_imag = transform(turn_real, turn_imag, fore, back)
        total[0] = total[0] + dpsi_real
        total[1] = total[1] + dpsi_imag

    @pl.when(plan_ref[0, step + 1] != plan_ref[0, step])
    def _():
        sums_ref[0] = summed[:, :, : sums_ref.shape[3], :].astype(jnp.bfloat16)

    @pl.when(step == last_step)
    def _():
        total_ref[...] = total[...]


def visiting_plan(targets, offsets, nbatch):
    local_rows = targets.shape[0]
    steps = local_rows + nbatch
    serial = jnp.arange(local_rows, dtype=jnp.int32)
    ahead = (targets[None, :] < targets[:, None]) | (
        (targets[None, :] == targets[:, None]) & (serial[None, :] < serial[:, None])
    )
    rank = jnp.sum(ahead.astype(jnp.int32), axis=1)
    rows = jnp.arange(nbatch, dtype=jnp.int32)
    opening = rows + jnp.sum((targets[None, :] < rows[:, None]).astype(jnp.int32), axis=1)
    count = jnp.arange(steps, dtype=jnp.int32)
    tile = jnp.sum((opening[None, :] <= count[:, None]).astype(jnp.int32), axis=1) - 1
    opens = jnp.any(opening[None, :] == count[:, None], axis=1)
    visit = 1 - opens.astype(jnp.int32)
    wanted = jnp.minimum(count - tile - visit, local_rows - 1)
    chosen = (rank[None, :] == wanted[:, None]).astype(jnp.int32)
    table = jnp.stack([serial, offsets[:, 0], offsets[:, 1]])
    picked = jnp.sum(chosen[None] * table[:, None, :], axis=2)
    plan = jnp.concatenate([tile[None], visit[None], picked], 0)
    return jnp.pad(plan, ((0, 0), (0, 1)), constant_values=-1)


def visit_all(plan, column, probe_wave, intensities, tables_of):
    nbatch, slices, _, tile_rows, tile_cols = column.shape
    extent = probe_wave.shape[-1]
    fore, back, prop = tables_of
    steps = plan.shape[1] - 1
    local_rows = intensities.shape[0]
    tile_block = (1, slices, 2, tile_rows, tile_cols)

    def whole(shape):
        return pl.BlockSpec(
            shape, lambda i, plan_ref: (0,) * len(shape), pipeline_mode=pl.Buffered(1)
        )

    return pl.pallas_call(
        visit_kernel,
        out_shape=(
            jax.ShapeDtypeStruct(column.shape, jnp.bfloat16),
            jax.ShapeDtypeStruct((2, extent, extent), jnp.float32),
        ),
        grid_spec=pltpu.PrefetchScalarGridSpec(
            num_scalar_prefetch=1,
            grid=(steps,),
            in_specs=[
                pl.BlockSpec(tile_block, lambda i, plan_ref: (plan_ref[0, i], 0, 0, 0, 0)),
                pl.BlockSpec((1, extent, extent), lambda i, plan_ref: (plan_ref[2, i], 0, 0)),
                whole(probe_wave.shape),
                whole(fore.shape),
                whole(back.shape),
                whole(prop.shape),
            ],
            out_specs=(
                pl.BlockSpec(tile_block, lambda i, plan_ref: (plan_ref[0, i], 0, 0, 0, 0)),
                pl.BlockSpec((2, extent, extent), lambda i, plan_ref: (0, 0, 0)),
            ),
            scratch_shapes=[
                pltpu.VMEM((slices, 2, tile_rows + sublanes, tile_cols), jnp.float32),
                pltpu.VMEM((slices, 2, tile_rows + sublanes, tile_cols), jnp.float32),
                pltpu.VMEM((slices, 2, extent, extent), jnp.float32),
                pltpu.VMEM((slices, 2, extent, extent), jnp.bfloat16),
                pltpu.VMEM((2, extent, extent), jnp.float32),
            ],
        ),
        compiler_params=pltpu.CompilerParams(
            dimension_semantics=("arbitrary",), vmem_limit_bytes=48 * 1024 * 1024
        ),
        cost_estimate=pl.CostEstimate(
            flops=local_rows * (3 * slices) * 16 * extent**3,
            bytes_accessed=2 * column.size * 2 + intensities.size * 4,
            transcendentals=0,
        ),
    )(plan, column, intensities, probe_wave, fore, back, prop)


def tv_local(padded):
    corner_cells = padded[:, :, :-1, :-1]
    down_diff = padded[:, :, 1:, :-1] - corner_cells
    right_diff = padded[:, :, :-1, 1:] - corner_cells
    weight = 1.0 / jnp.sqrt(
        jnp.sum(down_diff * down_diff + right_diff * right_diff, axis=1, keepdims=True) + tv_smooth
    )
    flow_down = weight * down_diff
    flow_right = weight * right_diff
    return (
        flow_down[:, :, :-1, 1:]
        + flow_right[:, :, 1:, :-1]
        - flow_down[:, :, 1:, 1:]
        - flow_right[:, :, 1:, 1:]
    )


def on_device(object_field, probe_wave, intensities, owner_rows, offsets):
    extent = probe_wave.shape[-1]
    nbatch = lax.axis_size("batch")
    column = lax.all_gather(object_field.astype(jnp.bfloat16), "batch", axis=0, tiled=False)
    padded = extended(object_field, (("batch", 2), ("tile", 3)), 1)
    plan = visiting_plan(owner_rows[:, 0], offsets, nbatch)
    cos_table, sin_table, prop_real, prop_imag = tables(extent)
    fore = jnp.concatenate(
        [
            jnp.concatenate([cos_table, -sin_table], 1),
            jnp.concatenate([sin_table, cos_table], 1),
        ],
        0,
    )
    back = jnp.concatenate(
        [
            jnp.concatenate([cos_table, sin_table], 1),
            jnp.concatenate([-sin_table, cos_table], 1),
        ],
        0,
    )
    prop = jnp.stack([prop_real, prop_imag])
    sums, probe_local = visit_all(plan, column, probe_wave, intensities, (fore, back, prop))
    returned = lax.all_to_all(sums, "batch", split_axis=0, concat_axis=0, tiled=True)
    probe_total = lax.psum(probe_local, ("batch", "tile"))
    field_grad = jnp.sum(returned.astype(jnp.float32), axis=0)
    new_object = object_field - update_rate * (field_grad + tv_weight * tv_local(padded))
    new_probe = probe_wave.astype(jnp.float32) - probe_rate * probe_total
    return (new_object, new_probe)


def solution(mesh):
    return jax.shard_map(
        on_device,
        mesh=mesh,
        in_specs=(
            P(None, None, "batch", "tile"),
            P(),
            P(("batch", "tile"), None, None),
            P(("batch", "tile"), None),
            P(("batch", "tile"), None),
        ),
        out_specs=(P(None, None, "batch", "tile"), P()),
        check_vma=False,
    )
```

time: 1390 us -> 435 us (0.31)
  local copies, waits for them, and re-layouts: 664 us -> 3.94 us
  loops' own time: 121 us -> 0 us
  other arithmetic: 143 us -> 30 us
  Pallas kernels: 0 us -> 91.7 us
  waiting for transfers between devices: 352 us -> 283 us
  matrix products: 64.9 us -> 0 us
    dynamic_update_slice x96 -> x0, local copies, waits for them, and re-layouts: 392 us -> none  [the longest x64 375 us: add_slot(): lax.dynamic_update_slice(field_grad, current + returned[slot_idx].astype(...]
    ppermute x2, waiting for transfers between devices: 176 us -> 2.34 us  [extended(): before = lax.ppermute(last, axis, up)]
    another operation x3 -> x0, loops' own time: 121 us -> none  [the longest x1 118 us: on_device(): lax.fori_loop(0, slots_all, add_slot, jnp.zeros(object_field.shape, jnp.f...]
    dynamic_slice x160 -> x0, local copies, waits for them, and re-layouts: 119 us -> none  [the longest x64 67.5 us: add_slot(): current = lax.dynamic_slice(field_grad, start, patch_shape)]
    ppermute x2, waiting for transfers between devices: 0.01 us -> 102 us  [extended(): after = lax.ppermute(first, axis, down)]
    pallas_call x0 -> x1, Pallas kernels: none -> 91.7 us  [visit_all(): pl.pallas_call(visit_kernel, out_shape=(jax.ShapeDtypeStruct(column.shape...]
    convert_element_type x208 -> x1, other arithmetic: 67.9 us -> 0.07 us  [visiting_plan(): chosen = (rank[None, :] == wanted[:, None]).astype(jnp.int32)]
    gather x48 -> x0, local copies, waits for them, and re-layouts: 67.5 us -> none
  transfers between devices with their start and end apart: 8 -> 7, of which waited for: 3 -> 6; matrix products, arithmetic and copies ran while one was open for 25% -> 5% of each run, Pallas kernels for 0% -> 0%
where the time goes in v1:
time: 435 us; the launch traced here: 433 us
  waiting for transfers between devices  283 us (65%)
  Pallas kernels  91.7 us (21%)
  other arithmetic  30 us (7%)
  between operations  14.2 us (3%)
  starting transfers between devices  9.5 us (2%)
    psum x1, waiting for transfers between devices, on_device(): probe_total = lax.psum(probe_local, ('batch', 'tile'))  123 us
    ppermute x2, waiting for transfers between devices, extended(): after = lax.ppermute(first, axis, down)  102 us
    pallas_call x1, Pallas kernels, visit_all(): pl.pallas_call(visit_kernel, out_shape=(jax.ShapeDtypeStruct(column.shape...  91.7 us
    all_gather x1, waiting for transfers between devices, on_device(): lax.all_gather(object_field.astype(jnp.bfloat16), 'batch', axis=0, tiled=...  55.8 us
  transfers between devices with their start and end apart: 7, of which 6 were waited for; matrix products, arithmetic and copies ran while one was open for 5% of the time, Pallas kernels for 0%

profile of v1, /device:TPU:12, one launch (start us, length us, event | category | flops | bytes accessed | tf_op | source)
XLA Modules:
  0.0 432.7 jit_solution(8699812796099642047)
XLA Ops:
  7.2 2.8 convert_element_type.93
  10.1 0.1 convert_reduce_fusion.3
  10.4 0.2 convert_reduce_fusion.1
  10.7 0.1 multiply_reduce_fusion
  10.8 1.0 fusion.15
  11.8 1.1 multiply_convert_fusion
  12.9 1.0 fusion.11
  14.1 55.8 %all-gather.3.cloned.1.call-done = bf16[16,2,384,384]{3,2,1,0:T(8,128)(2,1)} async-done(((bf16[2,2,384,384]{3,2,1,0:T(8,128)(2,1)}), bf16[16,2,384,384]{3,2,1,0:T(8,128)(2,1)}) %all-gather.3.cloned.1.call-update) | async-done | bytes 9437200 | tf_op jit(solution)/shard_map/all_gather | solution.py:257
  69.9 91.7 %shard_map.68 = (bf16[8,2,2,384,384]{4,3,2,1,0:T(8,128)(2,1)}, f32[2,256,256]{2,1,0:T(8,128)}) custom-call(s32[5,25]{1,0:T(8,128)S(1)} %pad.4.plan_ref, bf16[8,2,2,384,384]{4,3,2,1,0:T(8,128)(2,1)} %bitcast.10, f32[16,256,256]{2,1,0:T(8,128)} %measured_ref.1, bf16[2,256,256]{2,1,0:T(8,128)(2,1)S(1)} %copy-done, ...), custom_call_target="tpu_custom_call" | custom-call | flops 25769803776 | bytes 23068672 | tf_op jit(solution)/shard_map/pallas_call | solution.py:197
  161.6 6.0 %all-to-all-start = ((bf16[8,2,2,384,384]{4,3,2,1,0:T(8,128)(2,1)}), bf16[8,2,2,384,384]{4,3,2,1,0:T(8,128)(2,1)}, u32[]{:S(2)}, u32[]{:S(2)}) async-start(bf16[8,2,2,384,384]{4,3,2,1,0:T(8,128)(2,1)} %get-tuple-element.4), calls=%async_computation | async-start | bytes 18874368 | tf_op jit(solution)/shard_map/all_to_all | solution.py:277
  167.6 1.2 collective-permute-start.1
  168.8 100.8 %collective-permute-done.1 = f32[2,2,1,384]{3,1,2,0:T(2,128)S(1)} collective-permute-done((f32[2,2,1,384]{3,1,2,0:T(2,128)S(1)}, f32[2,2,1,384]{3,1,2,0:T(2,128)S(1)}, u32[]{:S(2)}, u32[]{:S(2)}) %collective-permute-start.1) | collective-permute-done | bytes 6176 | tf_op jit(solution)/shard_map/ppermute | solution.py:25
  269.7 1.2 collective-permute-done
  270.9 1.2 pad_maximum_fusion.3
  272.1 1.5 copy.29
  273.6 1.6 collective-permute-start.2
  275.1 0.3 copy.31
  275.5 0.7 collective-permute-start.3
  276.1 1.1 collective-permute-done.2
  277.2 1.2 copy.30
  278.4 0.9 collective-permute-done.3
  279.3 0.3 copy.32
  279.6 2.2 maximum_maximum_fusion
  281.8 1.4 add_reduce_fusion
  283.2 0.4 copy-done.2
  283.5 1.4 add_rsqrt_fusion
  284.9 6.6 %broadcast_multiply_fusion.1 = (f32[2,2,385,385]{3,2,1,0:T(8,128)}, f32[2,2,385,385]{3,2,1,0:T(8,128)}) fusion(f32[2,385,385]{2,1,0:T(8,128)} %add_rsqrt_fusion, f32[2,2,386,385]{3,2,1,0:T(8,128)} %copy-done.2, f32[2,2,386,1]{3,2,1,0:T(8,128)S(1)} %copy.32, f32[2,2,1,384]{3,2,1,0:T(1,128)S(1)} %copy.28, f32[2,2,384,384]{3,2,1,0:T(8,128)S(1)} %copy-done.1, ...), kind=kLoop, calls=%fused_computation.16 | loop fusion | flops 4150300 | bytes 13049960 | tf_op jit(solution)/shard_map/mul | solution.py:244
  291.5 123.5 %all-reduce.3.cloned.1.call-done = f32[2,256,256]{2,1,0:T(8,128)} async-done(((f32[2,256,256]{2,1,0:T(8,128)}), f32[2,256,256]{2,1,0:T(8,128)}) %all-reduce.3.cloned.1.call-update) | async-done | bytes 524304 | tf_op jit(solution)/shard_map/psum | solution.py:278
  415.0 1.9 multiply_subtract_fusion
  416.9 5.3 %convert_reduce_fusion = f32[2,2,384,384]{3,2,1,0:T(8,128)S(1)} fusion(bf16[8,2,2,384,384]{4,3,2,1,0:T(8,128)(2,1)} %all-to-all-done), kind=kLoop, calls=%fused_computation | loop fusion | flops 8847360 | bytes 11796480 | tf_op jit(solution)/shard_map/reduce_sum | solution.py:279
  422.2 0.2 copy-done.4
  422.4 3.4 fusion.4
  (36 shorter events, 0.6 us)
Async XLA Ops:
  7.2 2.9 copy-start.5
  7.2 2.9 copy-start.6
  7.2 62.7 %all-gather.3.cloned.1.call-start = ((), (), s32[]{:S(2)}) async-start(), calls=%async_computation.2 | async-start | bytes 10616832 | tf_op jit(solution)/shard_map/all_gather | solution.py:257
  10.0 59.9 %copy-start = (bf16[2,256,256]{2,1,0:T(8,128)(2,1)S(1)}, bf16[2,256,256]{2,1,0:T(8,128)(2,1)}, u32[]{:S(2)}) copy-start(bf16[2,256,256]{2,1,0:T(8,128)(2,1)} %probe_ref.1) | copy-start | bytes 786436
  161.6 6.0 %copy-start.1 = (f32[2,2,384,384]{3,2,1,0:T(8,128)S(1)}, f32[2,2,384,384]{3,2,1,0:T(8,128)}, u32[]{:S(2)}) copy-start(f32[2,2,384,384]{3,2,1,0:T(8,128)} %param.5) | copy-start | bytes 7077892
  161.6 255.3 %all-to-all-start = ((bf16[8,2,2,384,384]{4,3,2,1,0:T(8,128)(2,1)}), bf16[8,2,2,384,384]{4,3,2,1,0:T(8,128)(2,1)}, u32[]{:S(2)}, u32[]{:S(2)}) async-start(bf16[8,2,2,384,384]{4,3,2,1,0:T(8,128)(2,1)} %get-tuple-element.4), calls=%async_computation | async-start | bytes 18874368 | tf_op jit(solution)/shard_map/all_to_all | solution.py:277
  167.6 247.4 %all-reduce.3.cloned.1.call-start = ((), (), s32[]{:S(2)}) async-start(), calls=%async_computation.1 | async-start | bytes 1048576 | tf_op jit(solution)/shard_map/psum | solution.py:278
  167.6 102.1 %collective-permute-start.1 = (f32[2,2,1,384]{3,1,2,0:T(2,128)S(1)}, f32[2,2,1,384]{3,1,2,0:T(2,128)S(1)}, u32[]{:S(2)}, u32[]{:S(2)}) collective-permute-start(f32[2,2,1,384]{3,1,2,0:T(2,128)S(1)} %copy.34), channel_id=1, source_target_pairs={{4,0},{8,4},{12,8},{16,12},{20,16},{24,20},{28,24},{0,28},{5,1},{9... | collective-permute-start | bytes 18440 | tf_op jit(solution)/shard_map/ppermute | solution.py:25
  168.8 102.1 %collective-permute-start = (f32[2,2,1,384]{3,1,2,0:T(2,128)S(1)}, f32[2,2,1,384]{3,1,2,0:T(2,128)S(1)}, u32[]{:S(2)}, u32[]{:S(2)}) collective-permute-start(f32[2,2,1,384]{3,1,2,0:T(2,128)S(1)} %copy.33), channel_id=1, source_target_pairs={{0,4},{4,8},{8,12},{12,16},{16,20},{20,24},{24,28},{28,0},{1,5},{5... | collective-permute-start | bytes 18440 | tf_op jit(solution)/shard_map/ppermute | solution.py:24
  273.6 3.7 collective-permute-start.2
  275.5 3.9 collective-permute-start.3
  281.8 1.8 copy-start.2
  416.9 5.4 %copy-start.3 = (f32[2,2,385,385]{3,2,1,0:T(8,128)S(1)}, f32[2,2,385,385]{3,2,1,0:T(8,128)}, u32[]{:S(2)}) copy-start(f32[2,2,385,385]{3,2,1,0:T(8,128)} %get-tuple-element.8) | copy-start | bytes 7114804
  416.9 5.6 %copy-start.4 = (f32[2,2,385,385]{3,2,1,0:T(8,128)S(1)}, f32[2,2,385,385]{3,2,1,0:T(8,128)}, u32[]{:S(2)}) copy-start(f32[2,2,385,385]{3,2,1,0:T(8,128)} %get-tuple-element.9) | copy-start | bytes 7114804
Sparse Core Ops, SparseCore 0:
  10.4 59.3 all-gather.2
  285.0 129.8 all-reduce.2
